TPU v7x, 32 devices: a whole 2x2x4 slice. The times are simulated.
32 devices in a mesh: cell: 4 (over y, x), chan: 8 (over z, core).
Axes of the slice: x: 2, y: 2, z: 4, core: 2. Of those that a mesh axis runs over, the one named last changes fastest.
Arguments:
- slab: bfloat16 [32768, 8192], P('cell', 'chan'), may hold values from -6 to 6
- cell_factor: float32 [32, 32768], P(None, 'cell'), may hold values from -6 to 6
- chan_factor: float32 [32, 8192], P(None, 'chan'), may hold values from -6 to 6
- cell_mttkrp: float32 [32, 32768], P(None, 'cell'), may hold values from -12 to 12
- chan_mttkrp: float32 [32, 8192], P(None, 'chan'), may hold values from -12 to 12
- cell_gram_acc: float32 [32, 32], replicated, as said below
- chan_gram_acc: float32 [32, 32], replicated, as said below
Outputs:
- time_row: float32 [32], replicated
- new_cell_factor: float32 [32, 32768], P(None, 'cell')
- new_chan_factor: float32 [32, 8192], P(None, 'chan')
- new_cell_mttkrp: float32 [32, 32768], P(None, 'cell')
- new_chan_mttkrp: float32 [32, 8192], P(None, 'chan')
- new_cell_gram: float32 [32, 32], replicated
- new_chan_gram: float32 [32, 32], replicated
Inputs may be any that keep to these rules, and one draw needn't show every extreme that they name: `cell_gram_acc`: symmetric with a dominant positive diagonal. `chan_gram_acc`: symmetric with a dominant positive diagonal.
All inputs are finite; a program needn't handle non-finite values.
Results may differ from a plain program's by a relative error of at most 0.0033.
Values sent between devices are 32-bit elements; how exact they have to be, the bound alone decides.
No kernel may reach another device: no remote copies, remote signals or barrier semaphores. Data moves between devices by JAX's collectives and lax.ppermute only.
A program may use at most 64 MiB of HBM per device.

v0:
```python
import math
import jax
import jax.numpy as jnp
from jax import lax
from jax.sharding import PartitionSpec as P


def spd_solve(matrix, right):
    lower = jnp.linalg.cholesky(matrix)
    return jax.scipy.linalg.cho_solve((lower, True), right)


def body(slab, cell_factor, chan_factor, cell_mttkrp, chan_mttkrp, cell_gram_acc, chan_gram_acc):
    hi = lax.Precision.HIGHEST
    n_cell = lax.axis_size("cell")
    n_chan = lax.axis_size("chan")
    local_rows = slab.shape[0]
    local_cols = slab.shape[1]
    all_rows = local_rows * n_cell
    all_cols = local_cols * n_chan
    chan_low = chan_factor.astype(jnp.bfloat16)
    slab_chan = lax.dot_general(
        chan_low, slab, (((1,), (1,)), ((), ())), preferred_element_type=jnp.float32
    )
    rhs_part = jnp.sum(cell_factor * slab_chan, axis=1) / math.sqrt(all_rows * all_cols)
    cell_part = jnp.dot(cell_factor, cell_factor.T, precision=hi) / all_rows
    chan_part = jnp.dot(chan_factor, chan_factor.T, precision=hi) / all_cols
    rhs = lax.psum(rhs_part, ("cell", "chan"))
    cell_norm = lax.psum(cell_part, "cell")
    chan_norm = lax.psum(chan_part, "chan")
    time_row = spd_solve(cell_norm * chan_norm, rhs[:, None])[:, 0]
    outer = time_row[:, None] * time_row[None, :]
    new_cell_gram = cell_gram_acc + chan_norm * outer
    summed = lax.psum(slab_chan, "chan")
    new_cell_mttkrp = cell_mttkrp + time_row[:, None] * summed / math.sqrt(all_cols)
    new_cell_factor = spd_solve(new_cell_gram, new_cell_mttkrp)
    local_gram = jnp.dot(new_cell_factor, new_cell_factor.T, precision=hi) / all_rows
    new_norm = lax.psum(local_gram, "cell")
    cell_low = new_cell_factor.astype(jnp.bfloat16)
    slab_cell = jnp.dot(cell_low, slab, preferred_element_type=jnp.float32)
    cell_summed = lax.psum(slab_cell, "cell")
    new_chan_mttkrp = chan_mttkrp + time_row[:, None] * cell_summed / math.sqrt(all_rows)
    new_chan_gram = chan_gram_acc + new_norm * outer
    new_chan_factor = spd_solve(new_chan_gram, new_chan_mttkrp)
    return (
        time_row,
        new_cell_factor,
        new_chan_factor,
        new_cell_mttkrp,
        new_chan_mttkrp,
        new_cell_gram,
        new_chan_gram,
    )


def solution(mesh):
    placed = (
        P("cell", "chan"),
        P(None, "cell"),
        P(None, "chan"),
        P(None, "cell"),
        P(None, "chan"),
        P(),
        P(),
    )
    return jax.shard_map(
        body,
        mesh=mesh,
        in_specs=placed,
        out_specs=(
            P(),
            P(None, "cell"),
            P(None, "chan"),
            P(None, "cell"),
            P(None, "chan"),
            P(),
            P(),
        ),
        check_vma=False,
    )
```

profile of v0, /device:TPU:0, one launch (start us, length us, event | category | flops | bytes accessed | tf_op | source)
XLA Modules:
  0.0 202.9 jit_solution(13627783786792271417)
XLA Ops:
  7.3 12.4 %multiply_reduce_fusion = (f32[32]{0:T(128)S(1)}, f32[32,8192]{1,0:T(8,128)}) fusion(f32[32,8192]{1,0:T(8,128)} %param.9, bf16[8192,1024]{1,0:T(8,128)(2,1)} %param.8, f32[32,1024]{1,0:T(8,128)} %param.10), kind=kOutput, calls=%fused_computation.6 | convolution fusion | flops 537427968 | bytes 19005568 | tf_op jit(solution)/shard_map/dot_general | solution.py:22
  20.0 1.0 convolution_multiply_fusion.2
  21.0 30.4 %psum.43 = f32[32,32]{0,1:T(8,128)S(1)} all-reduce(f32[32,32]{0,1:T(8,128)S(1)} %convolution_multiply_fusion.1), channel_id=1, replica_groups=mesh['cell'=4,'chan'=8] {'chan'}, use_global_device_ids=true, to_apply=%region_1.0 | all-reduce | flops 1024 | bytes 8192 | tf_op jit(solution)/shard_map/psum | solution.py:30
  51.3 16.0 %psum.42 = f32[32,32]{0,1:T(8,128)S(1)} all-reduce(f32[32,32]{0,1:T(8,128)S(1)} %convolution_multiply_fusion.2), channel_id=1, replica_groups=mesh['cell'=4,'chan'=8] {'cell'}, use_global_device_ids=true, to_apply=%region_0.0 | all-reduce | flops 1024 | bytes 8192 | tf_op jit(solution)/shard_map/psum | solution.py:29
  67.4 2.9 %cholesky.59 = f32[32,32]{1,0:T(8,128)S(1)} custom-call(f32[32,32]{1,0:T(8,128)S(1)} %fusion.21), custom_call_target="Cholesky" | custom-call | tf_op jit(solution)/shard_map/jit(cholesky)/cholesky | solution.py:9
  70.4 0.6 compare_reduce_fusion.2
  71.0 0.7 fusion.4
  71.7 2.4 %custom-call.23 = f32[1,32,32]{1,2,0:T(8,128)S(1)} custom-call(f32[1,32,32]{2,1,0:T(8,128)S(1)} %fusion.4), custom_call_target="InvertDiagBlocksLowerTriangular" | custom-call | tf_op jit(solution)/shard_map/jit(_cho_solve)/triangular_solve | solution.py:10
  74.1 37.0 %psum.44 = f32[32]{0:T(128)S(1)} all-reduce(f32[32]{0:T(128)S(1)} %broadcast_multiply_fusion), channel_id=1, replica_groups=mesh['cell'=4,'chan'=8] {'cell','chan'}, use_global_device_ids=true, to_apply=%region_5.7 | all-reduce | flops 32 | bytes 256 | tf_op jit(solution)/shard_map/psum | solution.py:28
  111.7 2.9 %cholesky.70 = f32[32,32]{1,0:T(8,128)S(1)} custom-call(f32[32,32]{1,0:T(8,128)S(1)} %fusion.18), custom_call_target="Cholesky" | custom-call | tf_op jit(solution)/shard_map/jit(cholesky)/cholesky | solution.py:9
  115.3 0.7 fusion.5
  116.0 2.4 %custom-call.24 = f32[1,32,32]{1,2,0:T(8,128)S(1)} custom-call(f32[1,32,32]{2,1,0:T(8,128)S(1)} %fusion.5), custom_call_target="InvertDiagBlocksLowerTriangular" | custom-call | tf_op jit(solution)/shard_map/jit(_cho_solve)/triangular_solve | solution.py:10
  118.5 1.4 multiply_add_fusion
  119.9 1.0 fusion.16
  121.0 1.0 fusion.14
  122.0 1.0 convolution_multiply_fusion
  123.0 9.4 %fusion = f32[32,1024]{1,0:T(8,128)} fusion(bf16[8192,1024]{1,0:T(8,128)(2,1)} %param.8, f32[32,8192]{1,0:T(8,128)S(1)} %fusion.14), kind=kOutput, calls=%fused_computation.7 | convolution fusion | flops 537133056 | bytes 17956864 | tf_op jit(solution)/shard_map/dot_general | solution.py:40
  132.4 15.9 %psum.46 = f32[32,32]{0,1:T(8,128)S(1)} all-reduce(f32[32,32]{0,1:T(8,128)S(1)} %convolution_multiply_fusion), channel_id=1, replica_groups=mesh['cell'=4,'chan'=8] {'cell'}, use_global_device_ids=true, to_apply=%region_7.9 | all-reduce | flops 1024 | bytes 8192 | tf_op jit(solution)/shard_map/psum | solution.py:38
  148.5 2.9 %cholesky.81 = f32[32,32]{1,0:T(8,128)S(1)} custom-call(f32[32,32]{1,0:T(8,128)S(1)} %fusion.13), custom_call_target="Cholesky" | custom-call | tf_op jit(solution)/shard_map/jit(cholesky)/cholesky | solution.py:9
  152.1 0.7 fusion.6
  152.8 2.4 %custom-call.25 = f32[1,32,32]{1,2,0:T(8,128)S(1)} custom-call(f32[1,32,32]{2,1,0:T(8,128)S(1)} %fusion.6), custom_call_target="InvertDiagBlocksLowerTriangular" | custom-call | tf_op jit(solution)/shard_map/jit(_cho_solve)/triangular_solve | solution.py:10
  155.2 38.6 %all-reduce.5.cloned.1.call-done = f32[32,1024]{1,0:T(8,128)} async-done(((f32[32,1024]{1,0:T(8,128)}), f32[32,1024]{1,0:T(8,128)}) %all-reduce.5.cloned.1.call-update) | async-done | bytes 131088 | tf_op jit(solution)/shard_map/psum | solution.py:41
  193.8 1.0 multiply_add_fusion.1
  195.1 0.9 fusion.9
  (50 shorter events, 3.0 us)
Async XLA Ops:
  7.2 12.5 %copy-start.3 = (f32[32,1024]{1,0:T(8,128)S(1)}, f32[32,1024]{1,0:T(8,128)}, u32[]{:S(2)}) copy-start(f32[32,1024]{1,0:T(8,128)} %param.10) | copy-start | bytes 393220
  7.2 12.8 %copy-start.1 = (f32[32,8192]{1,0:T(8,128)S(1)}, f32[32,8192]{1,0:T(8,128)}, u32[]{:S(2)}) copy-start(f32[32,8192]{1,0:T(8,128)} %param.9) | copy-start | bytes 3145732
  7.2 104.3 %copy-start.10 = (f32[32,32]{1,0:T(8,128)S(1)}, f32[32,32]{1,0:T(8,128)}, u32[]{:S(2)}) copy-start(f32[32,32]{1,0:T(8,128)} %param.13) | copy-start | bytes 12292
  7.2 111.2 %copy-start.11 = (f32[32,32]{1,0:T(8,128)S(1)}, f32[32,32]{1,0:T(8,128)}, u32[]{:S(2)}) copy-start(f32[32,32]{1,0:T(8,128)} %param.14) | copy-start | bytes 12292
  7.2 111.3 %copy-start.4 = (f32[32,8192]{1,0:T(8,128)S(1)}, f32[32,8192]{1,0:T(8,128)}, u32[]{:S(2)}) copy-start(f32[32,8192]{1,0:T(8,128)} %param.11) | copy-start | bytes 3145732
  7.2 111.3 %all-reduce.3.cloned.1.call-start = ((), (), s32[]{:S(2)}) async-start(), calls=%async_computation | async-start | bytes 2097152 | tf_op jit(solution)/shard_map/psum | solution.py:34
  19.7 174.2 %all-reduce.5.cloned.1.call-start = ((), (), s32[]{:S(2)}) async-start(), calls=%async_computation.1 | async-start | bytes 262144 | tf_op jit(solution)/shard_map/psum | solution.py:41
  111.5 82.4 %copy-start.9 = (f32[32]{0:T(128)}, f32[32]{0:T(128)S(1)}, u32[]{:S(2)}) copy-start(f32[32]{0:T(128)S(1)} %convolution_bitcast_fusion) | copy-start | bytes 388
  111.7 20.7 %copy-start.7 = (f32[32,32]{1,0:T(8,128)}, f32[32,32]{1,0:T(8,128)S(1)}, u32[]{:S(2)}) copy-start(f32[32,32]{1,0:T(8,128)S(1)} %copy.18) | copy-start | bytes 12292
  119.9 32.8 %copy-start.2 = (f32[32,8192]{1,0:T(8,128)}, f32[32,8192]{1,0:T(8,128)S(1)}, u32[]{:S(2)}) copy-start(f32[32,8192]{1,0:T(8,128)S(1)} %multiply_add_fusion) | copy-start | bytes 3145732
  119.9 73.9 %copy-start.6 = (f32[32,1024]{1,0:T(8,128)S(1)}, f32[32,1024]{1,0:T(8,128)}, u32[]{:S(2)}) copy-start(f32[32,1024]{1,0:T(8,128)} %param.12) | copy-start | bytes 393220
  122.0 74.1 %copy-start = (f32[32,8192]{1,0:T(8,128)}, f32[32,8192]{1,0:T(8,128)S(1)}, u32[]{:S(2)}) copy-start(f32[32,8192]{1,0:T(8,128)S(1)} %fusion.14) | copy-start | bytes 3145732
  148.5 47.6 %copy-start.8 = (f32[32,32]{1,0:T(8,128)}, f32[32,32]{1,0:T(8,128)S(1)}, u32[]{:S(2)}) copy-start(f32[32,32]{1,0:T(8,128)S(1)} %copy.21) | copy-start | bytes 12292
  194.8 1.3 copy-start.5
Sparse Core Ops, SparseCore 0:
  19.8 61.7 all-reduce.2
  152.2 41.5 all-reduce.4
where the time goes:
time: 203 us
  blocking collectives  99.3 us (49%)
  waiting for transfers between devices  38.7 us (19%)
  matrix products  27.5 us (14%)
  other arithmetic  22.6 us (11%)
  between operations  14.3 us (7%)
    psum x1, waiting for transfers between devices, body(): cell_summed = lax.psum(slab_cell, 'cell')  38.6 us
    psum x1, blocking collectives, body(): rhs = lax.psum(rhs_part, ('cell', 'chan'))  37 us
    psum x1, blocking collectives, body(): chan_norm = lax.psum(chan_part, 'chan')  30.4 us
    psum x1, blocking collectives, body(): cell_norm = lax.psum(cell_part, 'cell')  16 us
    psum x1, blocking collectives, body(): new_norm = lax.psum(local_gram, 'cell')  15.9 us
    dot_general x1, matrix products, body(): lax.dot_general(chan_low, slab, (((1,), (1,)), ((), ())), preferred_eleme...  12.4 us
    another operation x9, other arithmetic, spd_solve(): lower = jnp.linalg.cholesky(matrix)  10.8 us
    dot_general x1, matrix products, body(): slab_cell = jnp.dot(cell_low, slab, preferred_element_type=jnp.float32)  9.41 us
  transfers between devices with their start and end apart: 2, of which 1 were waited for; matrix products, arithmetic and copies ran while one was open for 9% of the time, Pallas kernels for 0%

commit v1 on v0

--- a/solution.py
+++ b/solution.py
@@ -25,7 +25,7 @@
     rhs_part = jnp.sum(cell_factor * slab_chan, axis=1) / math.sqrt(all_rows * all_cols)
     cell_part = jnp.dot(cell_factor, cell_factor.T, precision=hi) / all_rows
     chan_part = jnp.dot(chan_factor, chan_factor.T, precision=hi) / all_cols
-    rhs = lax.psum(rhs_part, ("cell", "chan"))
+    rhs = lax.psum(lax.psum(rhs_part, "chan"), "cell")
     cell_norm = lax.psum(cell_part, "cell")
     chan_norm = lax.psum(chan_part, "chan")
     time_row = spd_solve(cell_norm * chan_norm, rhs[:, None])[:, 0]

time: 203 us -> 164 us (0.81)
  blocking collectives: 99.3 us -> 62.1 us
    psum x1 -> x0, blocking collectives: 37 us -> none  [body(): rhs = lax.psum(rhs_part, ('cell', 'chan'))]
  transfers between devices with their start and end apart: 2 -> 2, of which waited for: 1 -> 2; matrix products, arithmetic and copies ran while one was open for 9% -> 11% of each run, Pallas kernels for 0% -> 0%
where the time goes in v1:
time: 164 us
  blocking collectives  62.1 us (38%)
  waiting for transfers between devices  36.9 us (22%)
  matrix products  27.5 us (17%)
  other arithmetic  22.6 us (14%)
  between operations  14.3 us (9%)
    psum x1, waiting for transfers between devices, body(): cell_summed = lax.psum(slab_cell, 'cell')  36.6 us
    psum x1, blocking collectives, body(): chan_norm = lax.psum(chan_part, 'chan')  30.3 us
    psum x1, blocking collectives, body(): cell_norm = lax.psum(cell_part, 'cell')  16.2 us
    psum x1, blocking collectives, body(): new_norm = lax.psum(local_gram, 'cell')  15.5 us
    dot_general x1, matrix products, body(): lax.dot_general(chan_low, slab, (((1,), (1,)), ((), ())), preferred_eleme...  12.4 us
    another operation x9, other arithmetic, spd_solve(): lower = jnp.linalg.cholesky(matrix)  10.8 us
    dot_general x1, matrix products, body(): slab_cell = jnp.dot(cell_low, slab, preferred_element_type=jnp.float32)  9.41 us
    another operation x6, other arithmetic, spd_solve(): return jax.scipy.linalg.cho_solve((lower, True), right)  9.29 us
  transfers between devices with their start and end apart: 2, of which 2 were waited for; matrix products, arithmetic and copies ran while one was open for 11% of the time, Pallas kernels for 0%

profile of v1, /device:TPU:0, one launch (start us, length us, event | category | flops | bytes accessed | tf_op | source)
XLA Modules:
  0.0 163.9 jit_solution(3250509162322635334)
XLA Ops:
  7.3 12.4 %multiply_reduce_fusion = (f32[32]{0:T(128)S(1)}, f32[32,8192]{1,0:T(8,128)}) fusion(f32[32,8192]{1,0:T(8,128)} %param.9, bf16[8192,1024]{1,0:T(8,128)(2,1)} %param.8, f32[32,1024]{1,0:T(8,128)} %param.10), kind=kOutput, calls=%fused_computation.6 | convolution fusion | flops 537427968 | bytes 19005568 | tf_op jit(solution)/shard_map/dot_general | solution.py:22
  20.0 1.0 convolution_multiply_fusion.2
  21.0 30.3 %all-reduce = (f32[32,32]{0,1:T(8,128)S(1)}, f32[32]{0:T(128)S(1)}) all-reduce(f32[32,32]{0,1:T(8,128)S(1)} %convolution_multiply_fusion.1, f32[32]{0:T(128)S(1)} %broadcast_multiply_fusion), channel_id=1, replica_groups=mesh['cell'=4,'chan'=8] {'chan'}, use_global_device_ids=true, to_apply=%region_1.0 | all-reduce | flops 1056 | bytes 8448 | tf_op jit(solution)/shard_map/psum | solution.py:30
  51.3 16.2 %all-reduce.1 = (f32[32,32]{0,1:T(8,128)S(1)}, f32[32]{0:T(128)S(1)}) all-reduce(f32[32,32]{0,1:T(8,128)S(1)} %convolution_multiply_fusion.2, f32[32]{0:T(128)S(1)} %get-tuple-element.16), channel_id=1, replica_groups=mesh['cell'=4,'chan'=8] {'cell'}, use_global_device_ids=true, to_apply=%region_0.0 | all-reduce | flops 1056 | bytes 8448 | tf_op jit(solution)/shard_map/psum | solution.py:29
  67.6 2.9 %cholesky.59 = f32[32,32]{1,0:T(8,128)S(1)} custom-call(f32[32,32]{1,0:T(8,128)S(1)} %fusion.21), custom_call_target="Cholesky" | custom-call | tf_op jit(solution)/shard_map/jit(cholesky)/cholesky | solution.py:9
  70.6 0.6 compare_reduce_fusion.2
  71.2 0.7 fusion.4
  71.9 2.4 %custom-call.23 = f32[1,32,32]{1,2,0:T(8,128)S(1)} custom-call(f32[1,32,32]{2,1,0:T(8,128)S(1)} %fusion.4), custom_call_target="InvertDiagBlocksLowerTriangular" | custom-call | tf_op jit(solution)/shard_map/jit(_cho_solve)/triangular_solve | solution.py:10
  74.9 2.9 %cholesky.70 = f32[32,32]{1,0:T(8,128)S(1)} custom-call(f32[32,32]{1,0:T(8,128)S(1)} %fusion.18), custom_call_target="Cholesky" | custom-call | tf_op jit(solution)/shard_map/jit(cholesky)/cholesky | solution.py:9
  77.8 0.6 compare_reduce_fusion.1
  78.5 0.7 fusion.5
  79.1 2.5 %custom-call.24 = f32[1,32,32]{1,2,0:T(8,128)S(1)} custom-call(f32[1,32,32]{2,1,0:T(8,128)S(1)} %fusion.5), custom_call_target="InvertDiagBlocksLowerTriangular" | custom-call | tf_op jit(solution)/shard_map/jit(_cho_solve)/triangular_solve | solution.py:10
  81.9 1.4 multiply_add_fusion
  83.4 1.0 fusion.16
  84.4 1.0 fusion.14
  85.4 1.0 convolution_multiply_fusion
  86.4 9.4 %fusion = f32[32,1024]{1,0:T(8,128)} fusion(bf16[8192,1024]{1,0:T(8,128)(2,1)} %param.8, f32[32,8192]{1,0:T(8,128)S(1)} %fusion.14), kind=kOutput, calls=%fused_computation.7 | convolution fusion | flops 537133056 | bytes 17956864 | tf_op jit(solution)/shard_map/dot_general | solution.py:40
  95.8 15.5 %psum.54 = f32[32,32]{0,1:T(8,128)S(1)} all-reduce(f32[32,32]{0,1:T(8,128)S(1)} %convolution_multiply_fusion), channel_id=1, replica_groups=mesh['cell'=4,'chan'=8] {'cell'}, use_global_device_ids=true, to_apply=%region_8.10 | all-reduce | flops 1024 | bytes 8192 | tf_op jit(solution)/shard_map/psum | solution.py:38
  111.5 2.9 %cholesky.81 = f32[32,32]{1,0:T(8,128)S(1)} custom-call(f32[32,32]{1,0:T(8,128)S(1)} %fusion.13), custom_call_target="Cholesky" | custom-call | tf_op jit(solution)/shard_map/jit(cholesky)/cholesky | solution.py:9
  115.1 0.7 fusion.6
  115.8 2.4 %custom-call.25 = f32[1,32,32]{1,2,0:T(8,128)S(1)} custom-call(f32[1,32,32]{2,1,0:T(8,128)S(1)} %fusion.6), custom_call_target="InvertDiagBlocksLowerTriangular" | custom-call | tf_op jit(solution)/shard_map/jit(_cho_solve)/triangular_solve | solution.py:10
  118.2 36.6 %all-reduce.7.cloned.1.call-done = f32[32,1024]{1,0:T(8,128)} async-done(((f32[32,1024]{1,0:T(8,128)}), f32[32,1024]{1,0:T(8,128)}) %all-reduce.7.cloned.1.call-update) | async-done | bytes 131088 | tf_op jit(solution)/shard_map/psum | solution.py:41
  154.9 1.0 multiply_add_fusion.1
  156.2 0.9 fusion.9
  (49 shorter events, 2.6 us)
Async XLA Ops:
  7.2 12.5 %copy-start.3 = (f32[32,1024]{1,0:T(8,128)S(1)}, f32[32,1024]{1,0:T(8,128)}, u32[]{:S(2)}) copy-start(f32[32,1024]{1,0:T(8,128)} %param.10) | copy-start | bytes 393220
  7.2 12.8 %copy-start.1 = (f32[32,8192]{1,0:T(8,128)S(1)}, f32[32,8192]{1,0:T(8,128)}, u32[]{:S(2)}) copy-start(f32[32,8192]{1,0:T(8,128)} %param.9) | copy-start | bytes 3145732
  7.2 67.4 %copy-start.10 = (f32[32,32]{1,0:T(8,128)S(1)}, f32[32,32]{1,0:T(8,128)}, u32[]{:S(2)}) copy-start(f32[32,32]{1,0:T(8,128)} %param.13) | copy-start | bytes 12292
  7.2 74.4 %copy-start.11 = (f32[32,32]{1,0:T(8,128)S(1)}, f32[32,32]{1,0:T(8,128)}, u32[]{:S(2)}) copy-start(f32[32,32]{1,0:T(8,128)} %param.14) | copy-start | bytes 12292
  7.2 74.7 %copy-start.4 = (f32[32,8192]{1,0:T(8,128)S(1)}, f32[32,8192]{1,0:T(8,128)}, u32[]{:S(2)}) copy-start(f32[32,8192]{1,0:T(8,128)} %param.11) | copy-start | bytes 3145732
  7.2 74.7 %all-reduce.5.cloned.1.call-start = ((), (), s32[]{:S(2)}) async-start(), calls=%async_computation | async-start | bytes 2097152 | tf_op jit(solution)/shard_map/psum | solution.py:34
  19.7 135.2 %all-reduce.7.cloned.1.call-start = ((), (), s32[]{:S(2)}) async-start(), calls=%async_computation.1 | async-start | bytes 262144 | tf_op jit(solution)/shard_map/psum | solution.py:41
  74.6 80.2 %copy-start.9 = (f32[32]{0:T(128)}, f32[32]{0:T(128)S(1)}, u32[]{:S(2)}) copy-start(f32[32]{0:T(128)S(1)} %convolution_bitcast_fusion) | copy-start | bytes 388
  74.8 21.0 %copy-start.7 = (f32[32,32]{1,0:T(8,128)}, f32[32,32]{1,0:T(8,128)S(1)}, u32[]{:S(2)}) copy-start(f32[32,32]{1,0:T(8,128)S(1)} %copy.18) | copy-start | bytes 12292
  83.3 32.5 %copy-start.2 = (f32[32,8192]{1,0:T(8,128)}, f32[32,8192]{1,0:T(8,128)S(1)}, u32[]{:S(2)}) copy-start(f32[32,8192]{1,0:T(8,128)S(1)} %multiply_add_fusion) | copy-start | bytes 3145732
  83.3 71.5 %copy-start.6 = (f32[32,1024]{1,0:T(8,128)S(1)}, f32[32,1024]{1,0:T(8,128)}, u32[]{:S(2)}) copy-start(f32[32,1024]{1,0:T(8,128)} %param.12) | copy-start | bytes 393220
  85.4 71.7 %copy-start = (f32[32,8192]{1,0:T(8,128)}, f32[32,8192]{1,0:T(8,128)S(1)}, u32[]{:S(2)}) copy-start(f32[32,8192]{1,0:T(8,128)S(1)} %fusion.14) | copy-start | bytes 3145732
  111.5 45.6 %copy-start.8 = (f32[32,32]{1,0:T(8,128)}, f32[32,32]{1,0:T(8,128)S(1)}, u32[]{:S(2)}) copy-start(f32[32,32]{1,0:T(8,128)S(1)} %copy.21) | copy-start | bytes 12292
  155.8 1.3 copy-start.5
Sparse Core Ops, SparseCore 0:
  19.8 62.1 all-reduce.4
  115.3 39.5 all-reduce.6
